TPU v7x, 128 devices: a whole 4x4x4 slice. The times are simulated.
128 devices in a mesh: ray: 16 (over x, z), tile: 8 (over y, core).
Axes of the slice: x: 4, y: 4, z: 4, core: 2. Of those that a mesh axis runs over, the one named last changes fastest.
Arguments:
- data: float32 [64, 262144], P(None, ('ray', 'tile')), may hold values from -6 to 6
- sensitivity: bfloat16 [4096, 256, 512], P(('ray', 'tile')), may hold values from -0.25 to 0.25
- block_tiles: int32 [128, 8, 4], P(('ray', 'tile')), may hold values from 0 to 47
- block_bundles: int32 [128, 8, 4], P(('ray', 'tile')), may hold values from 0 to 7
Outputs:
- solution: float32 [64, 196608], P(None, 'tile')
- residual: float32 [64, 262144], P(None, ('ray', 'tile'))
Inputs may be any that keep to these rules, and one draw needn't show every extreme that they name: `block_tiles`: position of the block's tile among the 48 tiles of the owner given by the second index. `block_bundles`: the block's ray bundle among the device's 8 bundles.
All inputs are finite; a program needn't handle non-finite values.
Results may differ from a plain program's by a relative error of at most 0.004.
The roundings to bfloat16 on the way count: a program that leaves them out, or rounds other values in their place, can miss the bound.
Values may be sent and summed in bfloat16 or wider, within the bound.
A program may use at most 128 MiB of HBM per device.

v0:
```python
import jax
import jax.numpy as jnp
from jax import lax
from jax.sharding import PartitionSpec as P

RB = 256
CB = 512
ITERS = 2
BUND_DEV = 8
TILE_DEV = 48
eps_norm = 1e-06


def per_device(data, sensitivity, block_tiles, block_bundles):
    columns = data.shape[0]
    bundles = block_bundles.reshape(-1)
    requests = lax.all_to_all(block_tiles, "tile", split_axis=1, concat_axis=1, tiled=True).reshape(
        -1
    )
    bundle_onehot = (bundles[:, None] == jnp.arange(BUND_DEV, dtype=jnp.int32)[None, :]).astype(
        jnp.float32
    )
    owner_onehot = (requests[:, None] == jnp.arange(TILE_DEV, dtype=jnp.int32)[None, :]).astype(
        jnp.bfloat16
    )

    def fetch(field_bf):
        owned = field_bf.reshape(columns, TILE_DEV, CB)
        outgoing = jnp.take(owned, requests, axis=1)
        tiles = lax.all_to_all(outgoing, "tile", split_axis=1, concat_axis=1, tiled=True)
        return tiles

    def forward(field_bf):
        tiles = fetch(field_bf)
        partial_value = jnp.einsum(
            "cnk,nrk->ncr", tiles, sensitivity, preferred_element_type=jnp.float32
        )
        summed = jnp.einsum(
            "ncr,nb->cbr", partial_value, bundle_onehot, precision=lax.Precision.HIGHEST
        )
        return summed.reshape(columns, BUND_DEV * RB)

    def adjoint(rays_bf):
        picked = jnp.take(rays_bf.reshape(columns, BUND_DEV, RB), bundles, axis=1)
        terms = jnp.einsum(
            "cnr,nrk->cnk", picked, sensitivity, preferred_element_type=jnp.float32
        ).astype(jnp.bfloat16)
        arrived = lax.all_to_all(terms, "tile", split_axis=1, concat_axis=1, tiled=True)
        owned = jnp.einsum(
            "cnk,nt->ctk", arrived, owner_onehot, preferred_element_type=jnp.float32
        ).reshape(columns, TILE_DEV * CB)
        total = lax.psum(owned, "ray")
        return total

    def cell_norm(field):
        local = jnp.sum(field * field, axis=1)
        total = lax.psum(local, "tile")
        return jnp.sqrt(total + eps_norm)

    def ray_norm(rays):
        total = lax.psum(jnp.sum(rays * rays, axis=1), ("ray", "tile"))
        return jnp.sqrt(total + eps_norm)

    beta_now = ray_norm(data)
    rays_dir = data / beta_now[:, None]
    model_dir = adjoint(rays_dir.astype(jnp.bfloat16))
    alpha_now = cell_norm(model_dir)
    model_dir = model_dir / alpha_now[:, None]
    search = model_dir
    solution = jnp.zeros_like(model_dir)
    phi_bar = beta_now
    rho_bar = alpha_now
    for step in range(ITERS):
        rounded = model_dir.astype(jnp.bfloat16)
        rays_dir = forward(rounded) - alpha_now[:, None] * rays_dir
        beta_now = ray_norm(rays_dir)
        rays_dir = rays_dir / beta_now[:, None]
        rho_now = jnp.sqrt(rho_bar * rho_bar + beta_now * beta_now)
        cosine = rho_bar / rho_now
        sine_part = beta_now / rho_now
        phi_now = cosine * phi_bar
        phi_bar = sine_part * phi_bar
        solution = solution + (phi_now / rho_now)[:, None] * search
        if step + 1 < ITERS:
            model_dir = adjoint(rays_dir.astype(jnp.bfloat16)) - beta_now[:, None] * model_dir
            alpha_now = cell_norm(model_dir)
            model_dir = model_dir / alpha_now[:, None]
            theta_now = sine_part * alpha_now
            rho_bar = -cosine * alpha_now
            search = model_dir - (theta_now / rho_now)[:, None] * search
    residual = data - forward(solution.astype(jnp.bfloat16))
    return (solution, residual)


def solution(mesh):
    return jax.shard_map(
        per_device,
        mesh=mesh,
        in_specs=(
            P(None, ("ray", "tile")),
            P(("ray", "tile"), None, None),
            P(("ray", "tile"), None, None),
            P(("ray", "tile"), None, None),
        ),
        out_specs=(P(None, "tile"), P(None, ("ray", "tile"))),
        check_vma=False,
    )
```

profile of v0, /device:TPU:1, one launch (start us, length us, event | category | flops | bytes accessed | tf_op | source)
XLA Modules:
  0.0 731.6 jit_solution(17410393598439722855)
XLA Ops:
  8.5 6.0 all-to-all-start
  16.5 67.7 %psum.49 = f32[64]{0:T(128)S(1)} all-reduce(f32[64]{0:T(128)S(1)} %multiply_reduce_fusion.4), channel_id=1, replica_groups=mesh['ray'=16,'tile'=8] {'ray','tile'}, use_global_device_ids=true, to_apply=%region_1.0 | all-reduce | flops 64 | bytes 512 | tf_op jit(solution)/shard_map/psum | solution.py:61
  86.1 6.3 convert_bitcast_fusion.1
  92.4 4.4 all-to-all-start.1
  98.1 25.1 %all-to-all-done.1 = bf16[64,32,512]{2,0,1:T(8,128)(2,1)S(1)} async-done(((bf16[64,32,512]{2,0,1:T(8,128)(2,1)}), bf16[64,32,512]{2,0,1:T(8,128)(2,1)S(1)}, u32[]{:S(2)}, u32[]{:S(2)}) %all-to-all-start.1) | async-done | bytes 2097184 | tf_op jit(solution)/shard_map/all_to_all | solution.py:48
  124.9 6.3 copy.39
  131.3 119.1 %all-reduce.3.cloned.1.call-done = f32[64,24576]{1,0:T(8,128)} async-done(((f32[64,24576]{1,0:T(8,128)}), f32[64,24576]{1,0:T(8,128)}) %all-reduce.3.cloned.1.call-update) | async-done | bytes 6291472 | tf_op jit(solution)/shard_map/psum | solution.py:52
  250.4 3.3 multiply_reduce_fusion.1
  253.7 12.4 %psum.51 = f32[64]{0:T(128)S(1)} all-reduce(f32[64]{0:T(128)S(1)} %multiply_reduce_fusion.1), channel_id=1, replica_groups=mesh['ray'=16,'tile'=8] {'tile'}, use_global_device_ids=true, to_apply=%region_4.6 | all-reduce | flops 64 | bytes 512 | tf_op jit(solution)/shard_map/psum | solution.py:57
  266.1 3.2 fusion.37
  269.8 2.0 gather_fusion.1
  273.7 31.7 %all_to_all.30 = bf16[64,32,512]{2,0,1:T(8,128)(2,1)S(1)} all-to-all(bf16[64,32,512]{2,0,1:T(8,128)(2,1)S(1)} %select_bitcast_fusion.2), channel_id=1, replica_groups=mesh['ray'=16,'tile'=8] {'tile'}, dimensions={1} | all-to-all | bytes 4194304 | tf_op jit(solution)/shard_map/all_to_all | solution.py:30
  305.4 6.0 fusion.41
  311.5 2.0 fusion.6
  313.9 64.5 %psum.52 = f32[64]{0:T(128)S(1)} all-reduce(f32[64]{0:T(128)S(1)} %get-tuple-element.11), channel_id=1, replica_groups=mesh['ray'=16,'tile'=8] {'ray','tile'}, use_global_device_ids=true, to_apply=%region_6.0 | all-reduce | flops 64 | bytes 512 | tf_op jit(solution)/shard_map/psum | solution.py:61
  379.2 5.0 convert_bitcast_fusion
  384.2 30.1 %all_to_all.31 = bf16[64,32,512]{2,0,1:T(8,128)(2,1)S(1)} all-to-all(bf16[64,32,512]{2,0,1:T(8,128)(2,1)S(1)} %convert_bitcast_fusion), channel_id=1, replica_groups=mesh['ray'=16,'tile'=8] {'tile'}, dimensions={1} | all-to-all | bytes 4194304 | tf_op jit(solution)/shard_map/all_to_all | solution.py:48
  416.0 6.3 copy.41
  422.3 118.9 %all-reduce.5.cloned.1.call-done = f32[64,24576]{1,0:T(8,128)} async-done(((f32[64,24576]{1,0:T(8,128)}), f32[64,24576]{1,0:T(8,128)}) %all-reduce.5.cloned.1.call-update) | async-done | bytes 6291472 | tf_op jit(solution)/shard_map/psum | solution.py:52
  541.2 5.8 multiply_reduce_fusion
  547.0 12.4 %psum.54 = f32[64]{0:T(128)S(1)} all-reduce(f32[64]{0:T(128)S(1)} %multiply_reduce_fusion), channel_id=1, replica_groups=mesh['ray'=16,'tile'=8] {'tile'}, use_global_device_ids=true, to_apply=%region_9.12 | all-reduce | flops 64 | bytes 512 | tf_op jit(solution)/shard_map/psum | solution.py:57
  559.4 5.2 fusion.10
  565.1 2.0 gather_fusion.3
  568.9 31.7 %all_to_all.32 = bf16[64,32,512]{2,0,1:T(8,128)(2,1)S(1)} all-to-all(bf16[64,32,512]{2,0,1:T(8,128)(2,1)S(1)} %select_bitcast_fusion.1), channel_id=1, replica_groups=mesh['ray'=16,'tile'=8] {'tile'}, dimensions={1} | all-to-all | bytes 4194304 | tf_op jit(solution)/shard_map/all_to_all | solution.py:30
  600.7 6.0 fusion.42
  606.7 2.0 fusion.2
  609.1 64.8 %psum.55 = f32[64]{0:T(128)S(1)} all-reduce(f32[64]{0:T(128)S(1)} %multiply_reduce_fusion.2), channel_id=1, replica_groups=mesh['ray'=16,'tile'=8] {'ray','tile'}, use_global_device_ids=true, to_apply=%region_11.14 | all-reduce | flops 64 | bytes 512 | tf_op jit(solution)/shard_map/psum | solution.py:61
  673.9 7.4 %fusion.38 = (bf16[64,24576]{1,0:T(8,128)(2,1)S(1)}, f32[64,24576]{1,0:T(8,128)}) fusion(f32[64]{0:T(128)S(1)} %multiply_divide_fusion, f32[64]{0:T(128)S(1)} %add_sqrt_fusion, f32[64,24576]{1,0:T(8,128)} %all-reduce.5.cloned.1.call-done, f32[64]{0:T(128)S(1)} %get-tuple-element.13, f32[64]{0:T(128)S(1)} %get-tuple-element.9, ...), kind=kLoop, calls=%fused_computation.76 | loop fusion | flops 15728640 | bytes 22021632 | tf_op jit(solution)/shard_map/convert_element_type | solution.py:91
  681.7 2.0 gather_fusion.4
  685.6 30.1 %all_to_all.33 = bf16[64,32,512]{2,0,1:T(8,128)(2,1)S(1)} all-to-all(bf16[64,32,512]{2,0,1:T(8,128)(2,1)S(1)} %select_bitcast_fusion), channel_id=1, replica_groups=mesh['ray'=16,'tile'=8] {'tile'}, dimensions={1} | all-to-all | bytes 4194304 | tf_op jit(solution)/shard_map/all_to_all | solution.py:30
  715.7 6.0 fusion.43
  721.8 2.0 fusion
  (52 shorter events, 19.5 us)
Async XLA Ops:
  8.5 83.9 %all-to-all-start = ((s32[1,8,4]{2,0,1:T(1,128)}), s32[1,8,4]{2,0,1:T(1,128)S(1)}, u32[]{:S(2)}, u32[]{:S(2)}) async-start(s32[1,8,4]{2,0,1:T(1,128)} %copy.22), calls=%async_computation | async-start | bytes 8192 | tf_op jit(solution)/shard_map/all_to_all | solution.py:17
  92.4 30.8 %all-to-all-start.1 = ((bf16[64,32,512]{2,0,1:T(8,128)(2,1)}), bf16[64,32,512]{2,0,1:T(8,128)(2,1)S(1)}, u32[]{:S(2)}, u32[]{:S(2)}) async-start(bf16[64,32,512]{2,0,1:T(8,128)(2,1)} %convert_bitcast_fusion.1), calls=%async_computation.1 | async-start | bytes 4194304 | tf_op jit(solution)/shard_map/all_to_all | solution.py:48
  96.8 153.6 %all-reduce.3.cloned.1.call-start = ((), (), s32[]{:S(2)}) async-start(), calls=%async_computation.6 | async-start | bytes 12582912 | tf_op jit(solution)/shard_map/psum | solution.py:52
  131.2 410.0 %all-reduce.5.cloned.1.call-start = ((), (), s32[]{:S(2)}) async-start(), calls=%async_computation.7 | async-start | bytes 12582912 | tf_op jit(solution)/shard_map/psum | solution.py:52
  311.4 2.1 copy-start
  313.9 64.7 %copy-start.2 = (f32[64,2048]{1,0:T(8,128)}, f32[64,2048]{1,0:T(8,128)S(1)}, u32[]{:S(2)}) copy-start(f32[64,2048]{1,0:T(8,128)S(1)} %get-tuple-element.12) | copy-start | bytes 1572868
  606.7 2.1 copy-start.3
  721.7 2.1 copy-start.1
Sparse Core Ops, SparseCore 0:
  131.3 119.0 all-reduce.2
  422.4 118.6 all-reduce.4
where the time goes:
time: 733 us; the launch traced here: 732 us
  blocking collectives  346 us (47%)
  waiting for transfers between devices  263 us (36%)
  matrix products  38.8 us (5%)
  other arithmetic  35 us (5%)
  local copies, waits for them, and re-layouts  24.4 us (3%)
  between operations  14.3 us (2%)
  starting transfers between devices  10.4 us (1%)
    psum x2, waiting for transfers between devices, adjoint(): total = lax.psum(owned, 'ray')  238 us
    psum x3, blocking collectives, ray_norm(): total = lax.psum(jnp.sum(rays * rays, axis=1), ('ray', 'tile'))  197 us
    all_to_all x3, blocking collectives, fetch(): lax.all_to_all(outgoing, 'tile', split_axis=1, concat_axis=1, tiled=True)  93.6 us
    all_to_all x1, blocking collectives, adjoint(): lax.all_to_all(terms, 'tile', split_axis=1, concat_axis=1, tiled=True)  30.1 us
    all_to_all x1, waiting for transfers between devices, adjoint(): lax.all_to_all(terms, 'tile', split_axis=1, concat_axis=1, tiled=True)  25.1 us
    psum x2, blocking collectives, cell_norm(): total = lax.psum(local, 'tile')  24.9 us
    dot_general x3, matrix products, forward(): jnp.einsum('cnk,nrk->ncr', tiles, sensitivity, preferred_element_type=jnp...  18.1 us
    unnamed x15, local copies, waits for them, and re-layouts  15.1 us
  transfers between devices with their start and end apart: 4, of which 3 were waited for; matrix products, arithmetic and copies ran while one was open for 2% of the time, Pallas kernels for 0%

commit v1 on v0

--- a/solution.py
+++ b/solution.py
@@ -58,7 +58,9 @@
         return jnp.sqrt(total + eps_norm)
 
     def ray_norm(rays):
-        total = lax.psum(jnp.sum(rays * rays, axis=1), ("ray", "tile"))
+        total = jnp.sum(rays * rays, axis=1)
+        for over in ("ray", "tile"):
+            total = lax.psum(total, over)
         return jnp.sqrt(total + eps_norm)
 
     beta_now = ray_norm(data)

time: 733 us -> 687 us (0.937)
  blocking collectives: 346 us -> 304 us
    psum x3 -> x6, blocking collectives: 197 us -> 156 us  [ray_norm(): total = lax.psum(total, over)]
where the time goes in v1:
time: 687 us; the launch traced here: 686 us
  blocking collectives  304 us (44%)
  waiting for transfers between devices  259 us (38%)
  matrix products  38.8 us (6%)
  other arithmetic  35 us (5%)
  local copies, waits for them, and re-layouts  24.3 us (4%)
  between operations  14.3 us (2%)
  starting transfers between devices  9.77 us (1%)
    psum x2, waiting for transfers between devices, adjoint(): total = lax.psum(owned, 'ray')  234 us
    psum x6, blocking collectives, ray_norm(): total = lax.psum(total, over)  156 us
    all_to_all x3, blocking collectives, fetch(): lax.all_to_all(outgoing, 'tile', split_axis=1, concat_axis=1, tiled=True)  93 us
    all_to_all x1, blocking collectives, adjoint(): lax.all_to_all(terms, 'tile', split_axis=1, concat_axis=1, tiled=True)  29.6 us
    psum x2, blocking collectives, cell_norm(): total = lax.psum(local, 'tile')  25.1 us
    all_to_all x1, waiting for transfers between devices, adjoint(): lax.all_to_all(terms, 'tile', split_axis=1, concat_axis=1, tiled=True)  25.1 us
    dot_general x3, matrix products, forward(): jnp.einsum('cnk,nrk->ncr', tiles, sensitivity, preferred_element_type=jnp...  18.1 us
    unnamed x15, local copies, waits for them, and re-layouts  15.1 us
  transfers between devices with their start and end apart: 4, of which 3 were waited for; matrix products, arithmetic and copies ran while one was open for 2% of the time, Pallas kernels for 0%

profile of v1, /device:TPU:1, one launch (start us, length us, event | category | flops | bytes accessed | tf_op | source)
XLA Modules:
  0.0 685.5 jit_solution(15481982511001852928)
XLA Ops:
  8.5 6.0 all-to-all-start
  16.5 34.8 %psum.70 = f32[64]{0:T(128)S(1)} all-reduce(f32[64]{0:T(128)S(1)} %multiply_reduce_fusion.4), channel_id=1, replica_groups=mesh['ray'=16,'tile'=8] {'ray'}, use_global_device_ids=true, to_apply=%region_1.0 | all-reduce | flops 64 | bytes 512 | tf_op jit(solution)/shard_map/psum | solution.py:63
  51.3 19.1 %psum.71 = f32[64]{0:T(128)S(1)} all-reduce(f32[64]{0:T(128)S(1)} %psum.70), channel_id=1, replica_groups=mesh['ray'=16,'tile'=8] {'tile'}, use_global_device_ids=true, to_apply=%region_2.0 | all-reduce | flops 64 | bytes 512 | tf_op jit(solution)/shard_map/psum | solution.py:63
  72.2 6.3 convert_bitcast_fusion.1
  78.5 3.8 all-to-all-start.1
  83.5 25.1 %all-to-all-done.1 = bf16[64,32,512]{2,0,1:T(8,128)(2,1)S(1)} async-done(((bf16[64,32,512]{2,0,1:T(8,128)(2,1)}), bf16[64,32,512]{2,0,1:T(8,128)(2,1)S(1)}, u32[]{:S(2)}, u32[]{:S(2)}) %all-to-all-start.1) | async-done | bytes 2097184 | tf_op jit(solution)/shard_map/all_to_all | solution.py:48
  110.4 6.3 copy.39
  116.7 117.1 %all-reduce.3.cloned.1.call-done = f32[64,24576]{1,0:T(8,128)} async-done(((f32[64,24576]{1,0:T(8,128)}), f32[64,24576]{1,0:T(8,128)}) %all-reduce.3.cloned.1.call-update) | async-done | bytes 6291472 | tf_op jit(solution)/shard_map/psum | solution.py:52
  233.8 3.3 multiply_reduce_fusion.1
  237.1 12.4 %psum.73 = f32[64]{0:T(128)S(1)} all-reduce(f32[64]{0:T(128)S(1)} %multiply_reduce_fusion.1), channel_id=1, replica_groups=mesh['ray'=16,'tile'=8] {'tile'}, use_global_device_ids=true, to_apply=%region_5.7 | all-reduce | flops 64 | bytes 512 | tf_op jit(solution)/shard_map/psum | solution.py:57
  249.6 3.2 fusion.37
  253.3 2.0 gather_fusion.1
  257.1 31.7 %all_to_all.30 = bf16[64,32,512]{2,0,1:T(8,128)(2,1)S(1)} all-to-all(bf16[64,32,512]{2,0,1:T(8,128)(2,1)S(1)} %select_bitcast_fusion.2), channel_id=1, replica_groups=mesh['ray'=16,'tile'=8] {'tile'}, dimensions={1} | all-to-all | bytes 4194304 | tf_op jit(solution)/shard_map/all_to_all | solution.py:30
  288.8 6.0 fusion.41
  297.3 31.1 %psum.74 = f32[64]{0:T(128)S(1)} all-reduce(f32[64]{0:T(128)S(1)} %get-tuple-element.11), channel_id=1, replica_groups=mesh['ray'=16,'tile'=8] {'ray'}, use_global_device_ids=true, to_apply=%region_7.0 | all-reduce | flops 64 | bytes 512 | tf_op jit(solution)/shard_map/psum | solution.py:63
  328.4 20.0 %psum.75 = f32[64]{0:T(128)S(1)} all-reduce(f32[64]{0:T(128)S(1)} %psum.74), channel_id=1, replica_groups=mesh['ray'=16,'tile'=8] {'tile'}, use_global_device_ids=true, to_apply=%region_8.11 | all-reduce | flops 64 | bytes 512 | tf_op jit(solution)/shard_map/psum | solution.py:63
  349.2 5.0 convert_bitcast_fusion
  354.2 29.6 %all_to_all.31 = bf16[64,32,512]{2,0,1:T(8,128)(2,1)S(1)} all-to-all(bf16[64,32,512]{2,0,1:T(8,128)(2,1)S(1)} %convert_bitcast_fusion), channel_id=1, replica_groups=mesh['ray'=16,'tile'=8] {'tile'}, dimensions={1} | all-to-all | bytes 4194304 | tf_op jit(solution)/shard_map/all_to_all | solution.py:48
  385.5 6.3 copy.41
  391.8 117.2 %all-reduce.5.cloned.1.call-done = f32[64,24576]{1,0:T(8,128)} async-done(((f32[64,24576]{1,0:T(8,128)}), f32[64,24576]{1,0:T(8,128)}) %all-reduce.5.cloned.1.call-update) | async-done | bytes 6291472 | tf_op jit(solution)/shard_map/psum | solution.py:52
  509.0 5.8 multiply_reduce_fusion
  514.8 12.7 %psum.77 = f32[64]{0:T(128)S(1)} all-reduce(f32[64]{0:T(128)S(1)} %multiply_reduce_fusion), channel_id=1, replica_groups=mesh['ray'=16,'tile'=8] {'tile'}, use_global_device_ids=true, to_apply=%region_11.14 | all-reduce | flops 64 | bytes 512 | tf_op jit(solution)/shard_map/psum | solution.py:57
  527.5 5.2 fusion.10
  533.2 2.0 gather_fusion.3
  537.0 31.7 %all_to_all.32 = bf16[64,32,512]{2,0,1:T(8,128)(2,1)S(1)} all-to-all(bf16[64,32,512]{2,0,1:T(8,128)(2,1)S(1)} %select_bitcast_fusion.1), channel_id=1, replica_groups=mesh['ray'=16,'tile'=8] {'tile'}, dimensions={1} | all-to-all | bytes 4194304 | tf_op jit(solution)/shard_map/all_to_all | solution.py:30
  568.8 6.0 fusion.42
  577.2 31.1 %psum.78 = f32[64]{0:T(128)S(1)} all-reduce(f32[64]{0:T(128)S(1)} %multiply_reduce_fusion.2), channel_id=1, replica_groups=mesh['ray'=16,'tile'=8] {'ray'}, use_global_device_ids=true, to_apply=%region_13.16 | all-reduce | flops 64 | bytes 512 | tf_op jit(solution)/shard_map/psum | solution.py:63
  608.3 20.0 %psum.79 = f32[64]{0:T(128)S(1)} all-reduce(f32[64]{0:T(128)S(1)} %psum.78), channel_id=1, replica_groups=mesh['ray'=16,'tile'=8] {'tile'}, use_global_device_ids=true, to_apply=%region_14.17 | all-reduce | flops 64 | bytes 512 | tf_op jit(solution)/shard_map/psum | solution.py:63
  628.4 7.4 %fusion.38 = (bf16[64,24576]{1,0:T(8,128)(2,1)S(1)}, f32[64,24576]{1,0:T(8,128)}) fusion(f32[64]{0:T(128)S(1)} %multiply_divide_fusion, f32[64]{0:T(128)S(1)} %add_sqrt_fusion, f32[64,24576]{1,0:T(8,128)} %all-reduce.5.cloned.1.call-done, f32[64]{0:T(128)S(1)} %get-tuple-element.13, f32[64]{0:T(128)S(1)} %get-tuple-element.9, ...), kind=kLoop, calls=%fused_computation.76 | loop fusion | flops 15728640 | bytes 22021632 | tf_op jit(solution)/shard_map/convert_element_type | solution.py:93
  636.2 2.0 gather_fusion.4
  640.1 29.6 %all_to_all.33 = bf16[64,32,512]{2,0,1:T(8,128)(2,1)S(1)} all-to-all(bf16[64,32,512]{2,0,1:T(8,128)(2,1)S(1)} %select_bitcast_fusion), channel_id=1, replica_groups=mesh['ray'=16,'tile'=8] {'tile'}, dimensions={1} | all-to-all | bytes 4194304 | tf_op jit(solution)/shard_map/all_to_all | solution.py:30
  669.6 6.0 fusion.43
  (55 shorter events, 25.3 us)
Async XLA Ops:
  8.5 70.0 %all-to-all-start = ((s32[1,8,4]{2,0,1:T(1,128)}), s32[1,8,4]{2,0,1:T(1,128)S(1)}, u32[]{:S(2)}, u32[]{:S(2)}) async-start(s32[1,8,4]{2,0,1:T(1,128)} %copy.22), calls=%async_computation | async-start | bytes 8192 | tf_op jit(solution)/shard_map/all_to_all | solution.py:17
  78.5 30.1 %all-to-all-start.1 = ((bf16[64,32,512]{2,0,1:T(8,128)(2,1)}), bf16[64,32,512]{2,0,1:T(8,128)(2,1)S(1)}, u32[]{:S(2)}, u32[]{:S(2)}) async-start(bf16[64,32,512]{2,0,1:T(8,128)(2,1)} %convert_bitcast_fusion.1), calls=%async_computation.1 | async-start | bytes 4194304 | tf_op jit(solution)/shard_map/all_to_all | solution.py:48
  82.3 151.6 %all-reduce.3.cloned.1.call-start = ((), (), s32[]{:S(2)}) async-start(), calls=%async_computation.6 | async-start | bytes 12582912 | tf_op jit(solution)/shard_map/psum | solution.py:52
  116.6 392.4 %all-reduce.5.cloned.1.call-start = ((), (), s32[]{:S(2)}) async-start(), calls=%async_computation.7 | async-start | bytes 12582912 | tf_op jit(solution)/shard_map/psum | solution.py:52
  294.9 2.1 copy-start
  297.3 51.3 %copy-start.2 = (f32[64,2048]{1,0:T(8,128)}, f32[64,2048]{1,0:T(8,128)S(1)}, u32[]{:S(2)}) copy-start(f32[64,2048]{1,0:T(8,128)S(1)} %get-tuple-element.12) | copy-start | bytes 1572868
  574.8 2.1 copy-start.3
  675.7 2.1 copy-start.1
Sparse Core Ops, SparseCore 0:
  116.8 117.0 all-reduce.2
  392.0 117.0 all-reduce.4
